TPU v7x, 256 devices: a whole 4x4x8 slice. The times are simulated.
256 devices in a mesh: node: 2 (over z_lo), row: 128 (over x, z_hi, y, core).
Axes of the slice: x: 4, y: 4, z: 8 (z_hi: 4, z_lo: 2; z = z_hi * 2 + z_lo), core: 2. Of those that a mesh axis runs over, the one named last changes fastest.
Arguments:
- hamiltonian: float32 [256, 7, 128, 128], P('row'), may hold values from -0.09375 to 0.09375
- column_blocks: int32 [256, 7], P('row'), may hold values from 0 to 255, as said below
- start_basis: float32 [32768, 256], P('row'), may hold values from -48 to 48
- node_re: float32 [6], P('node'), may hold values from 1.5 to 2.5
- node_im: float32 [6], P('node'), may hold values from 0.5 to 1.5
- weight_re: float32 [6], P('node'), may hold values from 0.5 to 1.5
- weight_im: float32 [6], P('node'), may hold values from -1 to 1
- sweep_count: int32 [6], P('node'), may hold values from 1 to 2, as said below
Outputs:
- basis: float32 [32768, 256], P('row')
Inputs may be any that keep to these rules, and one draw needn't show every extreme that they name: `column_blocks`: tile 0 of row block b lies in column block b, tile 1 in b - 2 and tile 2 in b + 2, taken cyclically modulo 256; every other tile lies within 2 blocks of b, cyclically. `sweep_count`: some node takes 1 sweep and some node takes 2.
All inputs are finite; a program needn't handle non-finite values.
Results may differ from a plain program's by a relative error of at most 0.00022.
Values sent between devices are 32-bit elements; how exact they have to be, the bound alone decides.
A program may use at most 64 MiB of HBM per device.

v0:
```python
import math

import jax
import jax.numpy as jnp
from jax import lax
from jax.sharding import Mesh
from jax.sharding import PartitionSpec as P

REACH = 2
SWEEPS = 2
NS_ITERS = 2
ROW = ("row_0", "row_1", "row_2", "row_3")


def copy_for_each(value, axis):
    size = lax.axis_size(axis)
    return lax.all_to_all(
        jnp.broadcast_to(value[None], (size, *value.shape)), axis, 0, 0, tiled=True
    )


def of_everyone(value, axis):
    everything = copy_for_each(value, axis)
    return jnp.sum(everything, axis=0)


def extended_2(block, sides, width):
    for axis, dim in sides:
        count = lax.axis_size(axis)
        forward = [(i, i + 1) for i in range(count - 1)]
        forward.append((count - 1, 0))
        backward = [(target, source) for source, target in forward]
        low = lax.ppermute(
            lax.slice_in_dim(block, block.shape[dim] - width, None, axis=dim), axis, forward
        )
        high = lax.ppermute(lax.slice_in_dim(block, 0, width, axis=dim), axis, backward)
        block = jnp.concatenate([low, block, high], axis=dim)
    return block


def rows_for(lines, size):
    spare = -len(lines) % size
    return jnp.pad(lines, [(0, spare)] + [(0, 0)] * (lines.ndim - 1))


def laid_out(tiles, dim):
    dims = list(tiles.shape[1:])
    dims[dim] *= tiles.shape[0]
    return jnp.moveaxis(tiles, 0, dim).reshape(dims)


def gathered_by_axis(value, axes, dim):
    far, near = axes
    tiles = copy_for_each(copy_for_each(value, far), near)
    return laid_out(tiles.swapaxes(0, 1).reshape(-1, *value.shape), dim)


def in_blocks(value, dim, size):
    dims = value.shape
    tiles = value.reshape(*dims[:dim], size, dims[dim] // size, *dims[dim + 1 :])
    return jnp.moveaxis(tiles, dim, 0)


def sum_at_owner(value, axis, dim):
    size = lax.axis_size(axis)
    tiles = lax.all_to_all(in_blocks(value, dim, size), axis, 0, 0, tiled=True)
    return jnp.sum(tiles, axis=0)


def sum_by_axis(value, axes, dim):
    far, near = axes
    tiles = in_blocks(value, dim, lax.axis_size(far))
    nearer = sum_at_owner(tiles, near, dim + 1)
    arrived = lax.all_to_all(nearer, far, split_axis=0, concat_axis=0, tiled=True)
    return arrived.sum(axis=0)


def sum_by_parts(value, axes):
    lines = value.reshape(-1, value.shape[-1])
    padded = rows_for(lines, lax.axis_size(axes[0]) * lax.axis_size(axes[1]))
    whole = gathered_by_axis(sum_by_axis(padded, axes, 0), axes, 0)
    return lax.slice_in_dim(whole, 0, len(lines)).reshape(value.shape)


def apply_local(hamiltonian, local_cols, extended):
    breadth = extended.shape[1]
    count_blocks = hamiltonian.shape[0]
    tile_rows = hamiltonian.shape[2]
    blocks = extended.reshape(-1, tile_rows, breadth)
    summed = jnp.zeros((count_blocks, tile_rows, breadth), jnp.float32)
    for column in range(hamiltonian.shape[1]):
        picked = jnp.take(blocks, local_cols[:, column], axis=0)
        summed = summed + jnp.einsum(
            "bij,bjw->biw", hamiltonian[:, column], picked, precision=lax.Precision.HIGHEST
        )
    return summed.reshape(count_blocks * tile_rows, breadth)


def local_gram(vectors):
    return lax.dot_general(
        vectors, vectors, (((0,), (0,)), ((), ())), precision=lax.Precision.HIGHEST
    )


def orthonormal(gram_matrix):
    norm_value = jnp.sqrt(jnp.sum(gram_matrix * gram_matrix) + 1e-06)
    matrix_a = gram_matrix / norm_value
    identity = jnp.eye(gram_matrix.shape[0], dtype=jnp.float32)
    current = identity
    for repeat in range(NS_ITERS):
        middle = 1.5 * identity - 0.5 * jnp.dot(current, matrix_a, precision=lax.Precision.HIGHEST)
        matrix_a = jnp.dot(matrix_a, middle, precision=lax.Precision.HIGHEST)
        current = jnp.dot(middle, current, precision=lax.Precision.HIGHEST)
    return (current, norm_value)


def finish(vectors, gram_matrix, row_scale):
    mixing, norm_value = orthonormal(gram_matrix)
    return (
        row_scale * jnp.dot(vectors, mixing, precision=lax.Precision.HIGHEST) / jnp.sqrt(norm_value)
    )


def on_device(
    hamiltonian, column_blocks, start_basis, node_re, node_im, weight_re, weight_im, sweep_count
):
    count_blocks = hamiltonian.shape[0]
    tile_rows = hamiltonian.shape[2]
    devices_row = lax.axis_size(ROW)
    first_block = lax.axis_index(ROW) * count_blocks
    local_cols = (column_blocks - first_block + REACH + count_blocks * devices_row) % (
        count_blocks * devices_row
    )
    rim_rows = REACH * tile_rows
    row_scale = math.sqrt(start_basis.shape[0] * devices_row)
    modulus = node_re * node_re + node_im * node_im
    inverse_re = node_re / modulus
    inverse_im = -node_im / modulus
    power_re, power_im = (inverse_re, inverse_im)
    listed = []
    for degree in range(SWEEPS + 1):
        active = (sweep_count >= degree).astype(jnp.float32)
        listed.append(jnp.sum(active * (weight_re * power_re - weight_im * power_im)))
        power_re, power_im = (
            power_re * inverse_re - power_im * inverse_im,
            power_re * inverse_im + power_im * inverse_re,
        )
    coefficients = of_everyone(jnp.stack(listed), "node")
    krylov = start_basis
    filtered = coefficients[0] * start_basis
    for degree in range(1, SWEEPS + 1):
        extended = extended_2(krylov, ((ROW, 0),), rim_rows)
        krylov = apply_local(hamiltonian, local_cols, extended)
        filtered = filtered + coefficients[degree] * krylov
    gram_matrix = sum_by_parts(local_gram(filtered), (("row_0", "row_1", "row_2"), "row_3"))
    return finish(filtered, gram_matrix, row_scale)


def solution(mesh):
    finer = Mesh(
        mesh.devices.reshape(mesh.shape["node"], 4, 4, 4, 2),
        ("node", "row_0", "row_1", "row_2", "row_3"),
    )
    return jax.shard_map(
        on_device,
        mesh=finer,
        in_specs=(
            P(ROW, None, None, None),
            P(ROW, None),
            P(ROW, None),
            P("node"),
            P("node"),
            P("node"),
            P("node"),
            P("node"),
        ),
        out_specs=P(ROW, None),
        check_vma=False,
    )
```

profile of v0, /device:TPU:1, one launch (start us, length us, event | category | flops | bytes accessed | tf_op | source)
XLA Modules:
  0.0 111.3 jit_solution(1308503020939496351)
XLA Ops:
  0.0 2.7 %collective-permute-start = (f32[256,256]{1,0:T(8,128)}, f32[256,256]{1,0:T(8,128)S(1)}, u32[]{:S(2)}, u32[]{:S(2)}) collective-permute-start(f32[256,256]{1,0:T(8,128)} %param.12), channel_id=1, source_target_pairs={{0,1},{1,2},{2,3},{3,4},{4,5},{5,6},{6,7},{7,8},{8,9},{9,10},{10,1... | collective-permute-start | bytes 786440 | tf_op jit(solution)/shard_map/ppermute | solution.py:33
  3.2 0.7 copy-done.21
  4.2 0.6 compare_and_fusion.5
  5.3 0.6 compare_and_fusion.1
  6.6 0.6 pad_clamp_fusion
  7.2 0.6 fusion.81
  7.8 0.9 collective-permute-done.1
  8.7 1.0 pad_maximum_fusion
  13.2 0.7 gather_fusion.6
  13.9 0.6 copy-done.15
  15.0 0.6 copy-done.5
  16.1 0.6 copy-done.11
  17.2 0.6 copy-done.7
  18.3 0.7 copy-done.13
  21.6 10.0 %collective-permute-start.3 = (f32[256,256]{1,0:T(8,128)S(1)}, f32[256,256]{1,0:T(8,128)S(1)}, u32[]{:S(2)}, u32[]{:S(2)}) collective-permute-start(f32[256,256]{1,0:T(8,128)S(1)} %bitcast.98), channel_id=1, source_target_pairs={{1,0},{2,1},{3,2},{4,3},{5,4},{6,5},{7,6},{8,7},{9,8},{10,9},{11,1... | collective-permute-start | bytes 786440 | tf_op jit(solution)/shard_map/ppermute | solution.py:36
  31.6 0.6 copy-done.19
  32.2 0.7 fusion.78
  32.9 2.0 %pad_maximum_fusion.2 = f32[3]{0:T(128)S(1)} fusion(f32[1]{0:T(128)} %bitcast.2, f32[1]{0:T(128)} %bitcast.1, f32[1]{0:T(128)} %bitcast), kind=kLoop, calls=%fused_computation.151 | loop fusion | flops 6 | bytes 24 | tf_op jit(solution)/shard_map/stack | solution.py:148
  34.9 5.0 %all_to_all.26 = f32[2,1,3]{2,1,0:T(1,128)S(1)} all-to-all(f32[2,1,3]{2,1,0:T(1,128)S(1)} %broadcast_in_dim.15), channel_id=1, replica_groups=mesh['node'=2,'row_0'=4,'row_1'=4,'row_2'=4,'row_3'=2] {'node'}, dimensions={0} | all-to-all | bytes 48 | tf_op jit(solution)/shard_map/all_to_all | solution.py:17
  39.9 0.6 fusion.96
  42.9 0.7 gather_fusion.11
  43.6 0.7 gather_fusion.12
  44.3 1.4 %gather_fusion.13 = f32[2,128,256]{2,1,0:T(8,128)} fusion(f32[6,128,256]{2,1,0:T(8,128)S(1)} %bitcast.89, s32[1024]{0:T(1024)} %pad_clamp_fusion), kind=kCustom, calls=%fused_computation.13.clone | custom fusion | bytes 524296 | tf_op jit(solution)/shard_map/jit(_take)/gather | solution.py:92
  50.0 1.1 %fusion.3 = f32[2,256,128]{1,2,0:T(8,128)S(1)} fusion(f32[2,256,128]{1,2,0:T(8,128)S(1)} %convolution_add_fusion.1, f32[2,128,256]{2,1,0:T(8,128)S(1)} %copy-done.2, f32[]{:T(128)} %bitcast.16, pred[2]{0:T(512)(128)(4,1)S(1)} %copy-done.18, f32[2,7,128,128]{3,2,1,0:T(8,128)S(1)} %copy-done), kind=kOutput, calls=%fused_computation.21 | convolution fusion | flops 100859904 | bytes 918020 | tf_op jit(solution)/shard_map/bij,bjw->biw/dot_general | solution.py:93
  51.1 1.4 %bitcast_add_fusion = f32[256,256]{1,0:T(8,128)S(1)} fusion(f32[2,256,128]{1,2,0:T(8,128)S(1)} %fusion.3, f32[256,256]{1,0:T(8,128)S(1)} %copy-done.1, f32[]{:T(128)} %bitcast.5, f32[]{:T(128)} %bitcast.4, f32[2,256,128]{1,2,0:T(8,128)S(1)} %convolution_add_fusion.6), kind=kLoop, calls=%fused_computation.35 | loop fusion | flops 262144 | bytes 1048584 | tf_op jit(solution)/shard_map/add | solution.py:154
  52.5 0.6 fusion.97
  53.3 12.8 %all_to_all.27 = f32[2,64,2,256]{3,2,1,0:T(2,128)S(1)} all-to-all(f32[2,64,2,256]{3,2,1,0:T(2,128)S(1)} %bitcast.100), channel_id=1, replica_groups=mesh['node'=2,'row_0'=4,'row_1'=4,'row_2'=4,'row_3'=2] {'row_3'}, dimensions={0} | all-to-all | bytes 524288 | tf_op jit(solution)/shard_map/all_to_all | solution.py:66
  66.2 17.9 %all_to_all.28 = f32[64,2,256]{2,1,0:T(2,128)S(1)} all-to-all(f32[64,2,256]{2,1,0:T(2,128)S(1)} %reduce_sum.67), channel_id=1, replica_groups=mesh['node'=2,'row_0'=4,'row_1'=4,'row_2'=4,'row_3'=2] {'row_0','row_1',..., dimensions={0} | all-to-all | bytes 262144 | tf_op jit(solution)/shard_map/all_to_all | solution.py:74
  84.3 15.6 %all_to_all.29 = f32[64,2,256]{2,1,0:T(2,128)S(1)} all-to-all(f32[64,2,256]{2,1,0:T(2,128)S(1)} %broadcast_in_dim.16), channel_id=1, replica_groups=mesh['node'=2,'row_0'=4,'row_1'=4,'row_2'=4,'row_3'=2] {'row_0','row_1',..., dimensions={0} | all-to-all | bytes 262144 | tf_op jit(solution)/shard_map/all_to_all | solution.py:17
  100.0 6.6 %all_to_all.30 = f32[2,64,2,256]{3,2,1,0:T(2,128)S(1)} all-to-all(f32[2,64,2,256]{3,2,1,0:T(2,128)S(1)} %broadcast_in_dim.17), channel_id=1, replica_groups=mesh['node'=2,'row_0'=4,'row_1'=4,'row_2'=4,'row_3'=2] {'row_3'}, dimensions={0} | all-to-all | bytes 524288 | tf_op jit(solution)/shard_map/all_to_all | solution.py:17
  106.5 0.9 multiply_reduce_fusion
  110.2 1.1 fusion
  (106 shorter events, 19.0 us)
Async XLA Ops:
  0.0 7.8 %collective-permute-start = (f32[256,256]{1,0:T(8,128)}, f32[256,256]{1,0:T(8,128)S(1)}, u32[]{:S(2)}, u32[]{:S(2)}) collective-permute-start(f32[256,256]{1,0:T(8,128)} %param.12), channel_id=1, source_target_pairs={{0,1},{1,2},{2,3},{3,4},{4,5},{5,6},{6,7},{7,8},{8,9},{9,10},{10,1... | collective-permute-start | bytes 786440 | tf_op jit(solution)/shard_map/ppermute | solution.py:33
  2.7 6.0 %collective-permute-start.1 = (f32[256,256]{1,0:T(8,128)}, f32[256,256]{1,0:T(8,128)S(1)}, u32[]{:S(2)}, u32[]{:S(2)}) collective-permute-start(f32[256,256]{1,0:T(8,128)} %param.12), channel_id=1, source_target_pairs={{1,0},{2,1},{3,2},{4,3},{5,4},{6,5},{7,6},{8,7},{9,8},{10,9},{11,1... | collective-permute-start | bytes 786440 | tf_op jit(solution)/shard_map/ppermute | solution.py:36
  3.2 0.7 copy-start.21
  6.5 5.5 %copy-start.3 = (s32[1024]{0:T(1024)}, s32[1024]{0:T(1024)S(1)}, u32[]{:S(2)}) copy-start(s32[1024]{0:T(1024)S(1)} %pad_clamp_fusion.2) | copy-start | bytes 12292
  6.5 6.0 %copy-start.4 = (s32[1024]{0:T(1024)}, s32[1024]{0:T(1024)S(1)}, u32[]{:S(2)}) copy-start(s32[1024]{0:T(1024)S(1)} %pad_clamp_fusion.1) | copy-start | bytes 12292
  6.6 0.7 copy-start.22
  6.6 0.7 copy-start.23
  12.0 1.9 %copy-start = (f32[2,7,128,128]{3,2,1,0:T(8,128)S(1)}, f32[2,7,128,128]{3,2,1,0:T(8,128)}, u32[]{:S(2)}) copy-start(f32[2,7,128,128]{3,2,1,0:T(8,128)} %param.10) | copy-start | bytes 2752516
  13.9 0.7 copy-start.15
  15.0 0.6 copy-start.5
  16.1 0.6 copy-start.11
  17.2 0.6 copy-start.7
  18.3 0.7 copy-start.13
  19.5 0.6 copy-start.9
  20.1 0.6 copy-start.17
  20.6 10.9 %copy-start.25 = (f32[3]{0:T(128)S(1)}, f32[3]{0:T(128)}, u32[]{:S(2)}) copy-start(f32[3]{0:T(128)} %param.16) | copy-start | bytes 40
  20.6 10.9 %copy-start.26 = (f32[3]{0:T(128)S(1)}, f32[3]{0:T(128)}, u32[]{:S(2)}) copy-start(f32[3]{0:T(128)} %param.15) | copy-start | bytes 40
  21.1 19.4 %collective-permute-start.2 = (f32[256,256]{1,0:T(8,128)S(1)}, f32[256,256]{1,0:T(8,128)S(1)}, u32[]{:S(2)}, u32[]{:S(2)}) collective-permute-start(f32[256,256]{1,0:T(8,128)S(1)} %bitcast.97), channel_id=1, source_target_pairs={{0,1},{1,2},{2,3},{3,4},{4,5},{5,6},{6,7},{7,8},{8,9},{9,10},{10,1... | collective-permute-start | bytes 786440 | tf_op jit(solution)/shard_map/ppermute | solution.py:33
  21.6 19.0 %collective-permute-start.3 = (f32[256,256]{1,0:T(8,128)S(1)}, f32[256,256]{1,0:T(8,128)S(1)}, u32[]{:S(2)}, u32[]{:S(2)}) collective-permute-start(f32[256,256]{1,0:T(8,128)S(1)} %bitcast.98), channel_id=1, source_target_pairs={{1,0},{2,1},{3,2},{4,3},{5,4},{6,5},{7,6},{8,7},{9,8},{10,9},{11,1... | collective-permute-start | bytes 786440 | tf_op jit(solution)/shard_map/ppermute | solution.py:36
  31.5 0.7 copy-start.19
  31.5 0.7 copy-start.20
  31.6 0.7 copy-start.24
  44.3 1.4 %copy-start.16 = (pred[2]{0:T(512)(128)(4,1)S(1)}, pred[2]{0:T(512)(128)(4,1)}, u32[]{:S(2)}) copy-start(pred[2]{0:T(512)(128)(4,1)} %get-tuple-element.32) | copy-start | bytes 10
  45.7 0.6 copy-start.6
  46.3 0.6 copy-start.12
  47.0 0.6 copy-start.8
  47.6 0.7 copy-start.14
  48.3 0.6 copy-start.10
  48.9 0.9 copy-start.2
  49.3 0.6 copy-start.18
  50.0 1.1 %copy-start.1 = (f32[256,256]{1,0:T(8,128)S(1)}, f32[256,256]{1,0:T(8,128)}, u32[]{:S(2)}) copy-start(f32[256,256]{1,0:T(8,128)} %param.12) | copy-start | bytes 786436
where the time goes:
time: 112 us; the launch traced here: 111 us
  blocking collectives  57.8 us (52%)
  local copies, waits for them, and re-layouts  17.3 us (15%)
  starting transfers between devices  13.6 us (12%)
  matrix products  10.6 us (9%)
  other arithmetic  9.86 us (9%)
  between operations  1.28 us (1%)
    all_to_all x3, blocking collectives, copy_for_each(): lax.all_to_all(jnp.broadcast_to(value[None], (size, *value.shape)), axis,...  27.1 us
    all_to_all x1, blocking collectives, sum_by_axis(): lax.all_to_all(nearer, far, split_axis=0, concat_axis=0, tiled=True)  17.9 us
    all_to_all x1, blocking collectives, sum_at_owner(): tiles = lax.all_to_all(in_blocks(value, dim, size), axis, 0, 0, tiled=True)  12.8 us
    ppermute x2, starting transfers between devices, extended_2(): lax.ppermute(lax.slice_in_dim(block, 0, width, axis=dim), axis, backward)  10.5 us
    gather x14, local copies, waits for them, and re-layouts, apply_local(): picked = jnp.take(blocks, local_cols[:, column], axis=0)  9.1 us
    dot_general x14, matrix products, apply_local(): jnp.einsum('bij,bjw->biw', hamiltonian[:, column], picked, precision=lax....  7.2 us
    unnamed x54, local copies, waits for them, and re-layouts  6.69 us
    ppermute x2, starting transfers between devices, extended_2(): lax.ppermute(lax.slice_in_dim(block, block.shape[dim] - width, None, axis...  3.12 us
  transfers between devices with their start and end apart: 4, of which 1 were waited for; matrix products, arithmetic and copies ran while one was open for 6% of the time, Pallas kernels for 0%

commit v1 on v0

v1 whole, which is shorter than its diff:
```python
import functools
import itertools
import math

import jax
import jax.numpy as jnp
from jax import lax
from jax.experimental import pallas as pl
from jax.experimental.pallas import tpu as pltpu
from jax.sharding import Mesh
from jax.sharding import PartitionSpec as P

TILE = 128
REACH = 2
SWEEPS = 2
AXES = ("node", "x", "zh", "y", "core")
ROW = AXES[1:]
MESH = pl.DeviceIdType.MESH
F32 = jnp.float32
BF16 = jnp.bfloat16


def split(value):
    high = value.astype(BF16)
    return high, (value - high.astype(F32)).astype(BF16)


def product(left, right, dims=((1,), (0,))):
    def one(a, b):
        return lax.dot_general(a, b, (dims, ((), ())), preferred_element_type=F32)

    return one(left[0], right[0]) + (one(left[0], right[1]) + one(left[1], right[0]))


def pairwise(values):
    count = len(values)
    if count == 1:
        return values[0]
    if count == 2:
        return values[0] + values[1]
    return (values[0] + values[2]) + (values[1] + values[3])


def kernel(
    sizes,
    ham,
    cols,
    start,
    node_re,
    node_im,
    weight_re,
    weight_im,
    sweeps,
    out,
    ham_v,
    own,
    halo,
    krylov,
    halo1,
    band_hi,
    band_lo,
    coef,
    coef_in,
    part,
    rs_in,
    y_out,
    y_in,
    z_out,
    z_in,
    full,
    local_sem,
    halo_send,
    halo_recv,
    halo1_send,
    halo1_recv,
    coef_sem,
    rs_send,
    rs_recv,
    y_send,
    y_recv,
    z_send,
    z_recv,
    ag_send,
    ag_recv,
):
    nodes, nx, nzh, ny, cores = (sizes[a] for a in AXES)
    rows, width = start.shape
    piece = full.shape[0] // (nodes * nx * cores)
    me = {a: lax.axis_index(a) for a in AXES}
    ring = nx * nzh * ny * cores

    def away(**by):
        return {a: lax.rem(me[a] + by.get(a, 0) + sizes[a], sizes[a]) for a in AXES}

    position = ((me["x"] * nzh + me["zh"]) * ny + me["y"]) * cores + me["core"]

    def on_ring(step):
        at = lax.rem(position + step + ring, ring)
        return {
            "node": me["node"],
            "x": at // (nzh * ny * cores),
            "zh": lax.rem(at // (ny * cores), nzh),
            "y": lax.rem(at // cores, ny),
            "core": lax.rem(at, cores),
        }

    right, left = on_ring(1), on_ring(-1)

    ham_copy = pltpu.make_async_copy(ham, ham_v, local_sem.at[0])
    own_copy = pltpu.make_async_copy(start, own, local_sem.at[1])
    ham_copy.start()
    own_copy.start()

    rs_steps = [
        (dx, dc) for dx, dc in itertools.product(range(nx), range(cores)) if dx or dc
    ]
    ag_steps = [
        (dn, dx, dc)
        for dn, dx, dc in itertools.product(range(nodes), range(nx), range(cores))
        if dn or dx or dc
    ]
    peers = [left, right]
    peers += [away(node=dn, x=dx, core=dc) for dn, dx, dc in ag_steps]
    peers += [away(y=d) for d in range(1, ny)]
    peers += [away(zh=d) for d in range(1, nzh)]
    barrier = pltpu.get_barrier_semaphore()
    for peer in peers:
        pl.semaphore_signal(barrier, inc=1, device_id=peer, device_id_type=MESH)
    pl.semaphore_wait(barrier, len(peers))

    sent = []

    def send(src, dst, send_sem, recv_sem, peer):
        copy = pltpu.make_async_remote_copy(
            src_ref=src,
            dst_ref=dst,
            send_sem=send_sem,
            recv_sem=recv_sem,
            device_id=peer,
            device_id_type=MESH,
        )
        copy.start()
        sent.append(copy)
        return copy

    to_right = send(start, halo.at[0], halo_send.at[0], halo_recv.at[0], right)
    to_left = send(start, halo.at[1], halo_send.at[1], halo_recv.at[1], left)

    listed = [jnp.zeros((8, 128), F32) for _ in range(SWEEPS + 1)]
    for j in range(node_re.shape[0]):
        re, im = jnp.full((8, 128), node_re[j]), jnp.full((8, 128), node_im[j])
        w_re, w_im = jnp.full((8, 128), weight_re[j]), jnp.full((8, 128), weight_im[j])
        count = jnp.full((8, 128), sweeps[j])
        modulus = re * re + im * im
        inverse_re, inverse_im = re / modulus, -im / modulus
        power_re, power_im = inverse_re, inverse_im
        for degree in range(SWEEPS + 1):
            term = w_re * power_re - w_im * power_im
            listed[degree] = listed[degree] + jnp.where(count >= degree, term, 0.0)
            power_re, power_im = (
                power_re * inverse_re - power_im * inverse_im,
                power_re * inverse_im + power_im * inverse_re,
            )
    for degree, value in enumerate(listed):
        coef[8 * degree : 8 * degree + 8, :] = value
    coef_copy = send(coef, coef_in, coef_sem.at[0], coef_sem.at[1], away(node=1))

    ham_copy.wait()
    mine = rows // TILE
    blocks = mine * ring
    for a in range(mine):
        at = position * mine + a
        offset = [
            lax.rem(cols[a, k] - at + REACH + blocks, blocks) for k in range(ham.shape[1])
        ]
        for p in range(3 * mine):
            o = p - a + REACH - mine
            total = jnp.zeros((TILE, TILE), F32)
            if 0 <= o <= 2 * REACH:
                for k in range(ham.shape[1]):
                    fixed = (REACH, 0, 2 * REACH)
                    if k < 3:
                        if fixed[k] == o:
                            total = total + ham_v[a, k]
                    else:
                        total = total + jnp.where(offset[k] == o, 1.0, 0.0) * ham_v[a, k]
            high, low = split(total)
            place = (slice(a * TILE, (a + 1) * TILE), slice(p * TILE, (p + 1) * TILE))
            band_hi[place] = high
            band_lo[place] = low

    def band(side):
        at = slice(side * rows, (side + 1) * rows)
        return band_hi[:, at], band_lo[:, at]

    own_copy.wait()
    total = product(band(1), split(own[...]))
    to_right.wait_recv()
    total = total + product(band(0), split(halo[0]))
    to_left.wait_recv()
    total = total + product(band(2), split(halo[1]))
    krylov[...] = total
    to_right1 = send(krylov, halo1.at[0], halo1_send.at[0], halo1_recv.at[0], right)
    to_left1 = send(krylov, halo1.at[1], halo1_send.at[1], halo1_recv.at[1], left)
    coef_copy.wait_recv()
    scale = [
        (coef[8 * d : 8 * d + 8, :] + coef_in[8 * d : 8 * d + 8, :])[0:1, 0:1]
        for d in range(SWEEPS + 1)
    ]
    filtered = scale[0] * own[...] + scale[1] * total
    total = product(band(1), split(total))
    to_right1.wait_recv()
    total = total + product(band(0), split(halo1[0]))
    to_left1.wait_recv()
    total = total + product(band(2), split(halo1[1]))
    filtered = filtered + scale[2] * total

    f_split = split(filtered)
    half = width // 2
    first = tuple(v[:, :half] for v in f_split)
    last = tuple(v[:, half:] for v in f_split)
    top = product(first, f_split, ((0,), (0,)))
    part[0:half, :] = top[:, :half]
    part[half : 2 * half, :] = top[:, half:]
    part[2 * half :, :] = product(last, last, ((0,), (0,)))

    def piece_of(n, x, c):
        index = (n * nx + x) * cores + c
        return pl.ds(pl.multiple_of(index * piece, 8), piece)

    arriving = []
    for slot, (dx, dc) in enumerate(rs_steps):
        peer = away(x=dx, core=dc)
        theirs = piece_of(me["node"], peer["x"], peer["core"])
        arriving.append(
            send(part.at[theirs], rs_in.at[slot], rs_send.at[slot], rs_recv.at[slot], peer)
        )
    ours = piece_of(me["node"], me["x"], me["core"])
    value = part[ours, :]
    for slot, copy in enumerate(arriving):
        copy.wait_recv()
        value = value + rs_in[slot]

    def everywhere(value, axis, source, landing, send_sem, recv_sem):
        size = sizes[axis]
        if size == 1:
            return value
        source[...] = value
        copies = [
            send(source, landing.at[d - 1], send_sem.at[d - 1], recv_sem.at[d - 1], away(**{axis: d}))
            for d in range(1, size)
        ]
        for copy in copies:
            copy.wait_recv()
        return pairwise([value] + [landing[d - 1] for d in range(1, size)])

    value = everywhere(value, "y", y_out, y_in, y_send, y_recv)
    value = everywhere(value, "zh", z_out, z_in, z_send, z_recv)

    full[ours, :] = value
    for slot, (dn, dx, dc) in enumerate(ag_steps):
        send(full.at[ours], full.at[ours], ag_send.at[slot], ag_recv.at[slot], away(node=dn, x=dx, core=dc))
    for slot, (dn, dx, dc) in enumerate(ag_steps):
        source = away(node=-dn, x=-dx, core=-dc)
        theirs = piece_of(source["node"], source["x"], source["core"])
        pltpu.make_async_remote_copy(
            src_ref=full.at[theirs],
            dst_ref=full.at[theirs],
            send_sem=ag_send.at[slot],
            recv_sem=ag_recv.at[slot],
            device_id=source,
            device_id_type=MESH,
        ).wait_recv()

    corner = full[half : 2 * half, :]
    gram = jnp.concatenate(
        [
            jnp.concatenate([full[0:half, :], corner], axis=1),
            jnp.concatenate([corner.T, full[2 * half :, :]], axis=1),
        ],
        axis=0,
    )
    squares = jnp.sum(jnp.sum(gram * gram, axis=0, keepdims=True), axis=1, keepdims=True)
    norm = jnp.sqrt(squares + 1e-06)
    matrix = gram / norm
    m_split = split(matrix)
    square = product(m_split, m_split)
    mixed = product(split(square), split(0.0625 * square - 0.5625 * matrix))
    rows_at = lax.broadcasted_iota(jnp.int32, (width, width), 0)
    cols_at = lax.broadcasted_iota(jnp.int32, (width, width), 1)
    diagonal = jnp.where(rows_at == cols_at, 2.25, 0.0)
    mixed = mixed + (diagonal - 2.4375 * matrix + 1.6875 * square)
    result = product(f_split, split(mixed))
    out[...] = result * (math.sqrt(rows * ring) / jnp.sqrt(norm))

    for copy in sent:
        copy.wait_send()


def on_device(sizes, ham, cols, start, node_re, node_im, weight_re, weight_im, sweeps):
    rows, width = start.shape
    nodes, nx, nzh, ny, cores = (sizes[a] for a in AXES)
    packed = 3 * (width // 2)
    piece = packed // (nodes * nx * cores)
    anywhere = pl.BlockSpec(memory_space=pl.ANY)
    scalars = pl.BlockSpec(memory_space=pltpu.SMEM)
    vmem = pltpu.VMEM
    dma = pltpu.SemaphoreType.DMA
    others = nodes * nx * cores - 1
    near = nx * cores - 1
    return pl.pallas_call(
        functools.partial(kernel, sizes),
        out_shape=jax.ShapeDtypeStruct((rows, width), F32),
        in_specs=[anywhere, scalars, anywhere] + [scalars] * 5,
        out_specs=pl.BlockSpec(memory_space=pltpu.VMEM),
        scratch_shapes=[
            vmem(ham.shape, F32),
            vmem((rows, width), F32),
            vmem((2, rows, width), F32),
            vmem((rows, width), F32),
            vmem((2, rows, width), F32),
            vmem((rows, 3 * rows), BF16),
            vmem((rows, 3 * rows), BF16),
            vmem((8 * (SWEEPS + 1), 128), F32),
            vmem((8 * (SWEEPS + 1), 128), F32),
            vmem((packed, 128), F32),
            vmem((near, piece, 128), F32),
            vmem((piece, 128), F32),
            vmem((max(ny - 1, 1), piece, 128), F32),
            vmem((piece, 128), F32),
            vmem((max(nzh - 1, 1), piece, 128), F32),
            vmem((packed, 128), F32),
            dma((2,)),
            dma((2,)),
            dma((2,)),
            dma((2,)),
            dma((2,)),
            dma((2,)),
            dma((near,)),
            dma((near,)),
            dma((max(ny - 1, 1),)),
            dma((max(ny - 1, 1),)),
            dma((max(nzh - 1, 1),)),
            dma((max(nzh - 1, 1),)),
            dma((others,)),
            dma((others,)),
        ],
        compiler_params=pltpu.CompilerParams(
            collective_id=0, has_side_effects=True
        ),
    )(ham, cols, start, node_re, node_im, weight_re, weight_im, sweeps)


def build(finer):
    sizes = dict(finer.shape)
    return jax.shard_map(
        functools.partial(on_device, sizes),
        mesh=finer,
        in_specs=(
            P(ROW, None, None, None),
            P(ROW, None),
            P(ROW, None),
            P("node"),
            P("node"),
            P("node"),
            P("node"),
            P("node"),
        ),
        out_specs=P(ROW, None),
        check_vma=False,
    )


def solution(mesh):
    return build(Mesh(mesh.devices.reshape(mesh.shape["node"], 4, 4, 4, 2), AXES))
```

time: 112 us -> 51.8 us (0.46)
  blocking collectives: 57.8 us -> 0 us
  Pallas kernels: 0 us -> 50 us
  local copies, waits for them, and re-layouts: 17.3 us -> 1.67 us
  starting transfers between devices: 13.6 us -> 0 us
  matrix products: 10.6 us -> 0 us
  other arithmetic: 9.86 us -> 0 us
  between operations: 1.28 us -> 0.01 us
    all_to_all x5 -> x0, blocking collectives: 57.8 us -> none  [the longest x3 27.1 us: copy_for_each(): lax.all_to_all(jnp.broadcast_to(value[None], (size, *value.shape)), axis,...]
    pallas_call x0 -> x1, Pallas kernels: none -> 50 us  [on_device(): pl.pallas_call(functools.partial(kernel, sizes), out_shape=jax.ShapeDtype...]
    ppermute x4 -> x0, starting transfers between devices: 13.6 us -> none  [the longest x2 10.5 us: extended_2(): lax.ppermute(lax.slice_in_dim(block, 0, width, axis=dim), axis, backward)]
    dot_general x21 -> x0, matrix products: 10.6 us -> none  [the longest x14 7.2 us: apply_local(): jnp.einsum('bij,bjw->biw', hamiltonian[:, column], picked, precision=lax....]
    gather x14 -> x0, local copies, waits for them, and re-layouts: 9.1 us -> none  [apply_local(): picked = jnp.take(blocks, local_cols[:, column], axis=0)]
    unnamed x54 -> x1, local copies, waits for them, and re-layouts: 6.69 us -> 1.67 us
    and x4 -> x0, other arithmetic: 2.25 us -> none  [apply_local(): picked = jnp.take(blocks, local_cols[:, column], axis=0)]
    another operation x1 -> x0, other arithmetic: 2.01 us -> none  [on_device(): coefficients = of_everyone(jnp.stack(listed), 'node')]
  transfers between devices with their start and end apart: 4 -> 0, of which waited for: 1 -> 0; matrix products, arithmetic and copies ran while one was open for 6% -> 0% of each run, Pallas kernels for 0% -> 0%
where the time goes in v1:
time: 51.8 us; the launch traced here: 51.6 us
  Pallas kernels  50 us (97%)
  local copies, waits for them, and re-layouts  1.67 us (3%)
    pallas_call x1, Pallas kernels, on_device(): pl.pallas_call(functools.partial(kernel, sizes), out_shape=jax.ShapeDtype...  50 us
    unnamed x1, local copies, waits for them, and re-layouts  1.67 us

profile of v1, /device:TPU:1, one launch (start us, length us, event | category | flops | bytes accessed | tf_op | source)
XLA Modules:
  0.0 51.6 jit_solution(13464860998795496323)
XLA Ops:
  0.0 50.0 %shard_map.82 = f32[256,256]{1,0:T(8,128)} custom-call(f32[2,7,128,128]{3,2,1,0:T(8,128)} %ham.1, s32[2,7]{1,0:T(2,128)} %cols.1, f32[256,256]{1,0:T(8,128)} %start.1, f32[3]{0:T(128)} %node_re.1, f32[3]{0:T(128)} %node_im.1, f32[3]{0:T(128)} %weight_re.1, f32[3]{0:T(128)} %weight_im.1, s32[3]{0:T(128)} %sweeps.1), custom_call_target="tpu_custom_call" | custom-call | tf_op jit(solution)/shard_map/pallas_call | solution.py:311
  50.0 1.7 %copy.10 = f32[256,256]{1,0:T(8,128)} copy(f32[256,256]{1,0:T(8,128)} %shard_map.82) | data formatting | bytes 524288

commit v2 on v1

v2 whole, which is shorter than its diff:
```python
import functools
import itertools
import math

import jax
import jax.numpy as jnp
from jax import lax
from jax.experimental import pallas as pl
from jax.experimental.pallas import tpu as pltpu
from jax.sharding import Mesh
from jax.sharding import PartitionSpec as P

TILE = 128
REACH = 2
SWEEPS = 2
AXES = ("node", "x", "zh", "y", "core")
ROW = AXES[1:]
MESH = pl.DeviceIdType.MESH
F32 = jnp.float32
BF16 = jnp.bfloat16


def split(value):
    high = value.astype(BF16)
    return high, (value - high.astype(F32)).astype(BF16)


def product(left, right, dims=((1,), (0,))):
    def one(a, b):
        return lax.dot_general(a, b, (dims, ((), ())), preferred_element_type=F32)

    return one(left[0], right[0]) + (one(left[0], right[1]) + one(left[1], right[0]))


def pairwise(values):
    count = len(values)
    if count == 1:
        return values[0]
    if count == 2:
        return values[0] + values[1]
    return (values[0] + values[2]) + (values[1] + values[3])


def steps_over(sizes, axes):
    found = itertools.product(*(range(sizes[a]) for a in axes))
    return [dict(zip(axes, by)) for by in found if any(by)]


class Sum:
    def __init__(self, net, refs):
        self.net = net
        (
            self.part, self.rs_in, self.y_out, self.y_in, self.z_out, self.z_in, self.full,
            self.rs_sem, self.y_sem, self.z_sem, self.ag_sem,
        ) = refs
        self.steps = steps_over(net.sizes, ("x", "core"))
        self.everyone = steps_over(net.sizes, ("node", "x", "core"))
        self.rows = self.y_out.shape[0]

    def piece(self, at):
        index = 0
        for axis in ("node", "x", "core"):
            index = index * self.net.sizes[axis] + at[axis]
        return pl.ds(pl.multiple_of(index * self.rows, 8), self.rows)

    def scatter(self):
        self.copies = [
            self.net.send(
                self.part.at[self.piece(self.net.away(**by))],
                self.rs_in.at[slot],
                self.rs_sem.at[0, slot],
                self.rs_sem.at[1, slot],
                self.net.away(**by),
            )
            for slot, by in enumerate(self.steps)
        ]

    def scattered(self):
        value = self.part[self.piece(self.net.me), :]
        for slot, copy in enumerate(self.copies):
            copy.wait_recv()
            value = value + self.rs_in[slot]
        return value

    def share(self, value, axis, source, landing, sem):
        source[...] = value
        self.value = value
        self.landing = landing
        self.copies = [
            self.net.send(source, landing.at[d - 1], sem.at[0, d - 1], sem.at[1, d - 1], self.net.away(**{axis: d}))
            for d in range(1, self.net.sizes[axis])
        ]

    def shared(self):
        for copy in self.copies:
            copy.wait_recv()
        return pairwise([self.value] + [self.landing[d] for d in range(len(self.copies))])

    def to_y(self):
        self.share(self.scattered(), "y", self.y_out, self.y_in, self.y_sem)

    def to_z(self):
        self.share(self.shared(), "zh", self.z_out, self.z_in, self.z_sem)

    def gather(self):
        value = self.shared()
        ours = self.piece(self.net.me)
        self.full[ours, :] = value
        for slot, by in enumerate(self.everyone):
            self.net.send(
                self.full.at[ours],
                self.full.at[ours],
                self.ag_sem.at[0, slot],
                self.ag_sem.at[1, slot],
                self.net.away(**by),
            )

    def gathered(self):
        for slot, by in enumerate(self.everyone):
            source = self.net.away(**{a: -d for a, d in by.items()})
            theirs = self.full.at[self.piece(source)]
            self.net.copy(
                theirs, theirs, self.ag_sem.at[0, slot], self.ag_sem.at[1, slot], source
            ).wait_recv()


class Net:
    def __init__(self, sizes):
        self.sizes = sizes
        self.me = {a: lax.axis_index(a) for a in AXES}
        self.sent = []
        self.ring = math.prod(sizes[a] for a in ROW)
        me = self.me
        self.position = (
            (me["x"] * sizes["zh"] + me["zh"]) * sizes["y"] + me["y"]
        ) * sizes["core"] + me["core"]

    def away(self, **by):
        return {
            a: lax.rem(self.me[a] + by[a] + self.sizes[a], self.sizes[a]) if by.get(a) else self.me[a]
            for a in AXES
        }

    def on_ring(self, step):
        at = lax.rem(self.position + step + self.ring, self.ring)
        zh, y, core = (self.sizes[a] for a in ("zh", "y", "core"))
        return {
            "node": self.me["node"],
            "x": at // (zh * y * core),
            "zh": lax.rem(at // (y * core), zh),
            "y": lax.rem(at // core, y),
            "core": lax.rem(at, core),
        }

    def copy(self, src, dst, send_sem, recv_sem, peer):
        return pltpu.make_async_remote_copy(
            src_ref=src,
            dst_ref=dst,
            send_sem=send_sem,
            recv_sem=recv_sem,
            device_id=peer,
            device_id_type=MESH,
        )

    def send(self, *what):
        copy = self.copy(*what)
        copy.start()
        self.sent.append(copy)
        return copy


class Halo:
    def __init__(self, net, halo, sem):
        self.net, self.halo, self.sem = net, halo, sem
        self.near = (0, net.sizes["node"] - 1)
        me, last = net.me, {a: net.sizes[a] - 1 for a in AXES}
        first_in_line = (me["y"] == 0) & (me["core"] == 0)
        last_in_line = (me["y"] == last["y"]) & (me["core"] == last["core"])
        self.receives = (first_in_line, last_in_line)
        self.sends = (last_in_line, first_in_line)
        self.tile = halo.shape[2] // 2

    def target(self, slot):
        peer = self.net.on_ring(1 if slot == 0 else -1)
        return {**peer, "node": jnp.where(self.sends[slot], self.near[slot], self.net.me["node"])}

    def sending(self, slot):
        return jnp.logical_not(self.sends[slot]) | (self.net.me["node"] != self.near[slot])

    def unit(self, slot, c, j):
        return self.halo.at[slot, c, j * self.tile : (j + 1) * self.tile, :]

    def direct(self, src, slot, c, j):
        return self.net.copy(
            src, self.unit(slot, c, j), self.sem.at[0, slot, c, j], self.sem.at[1, slot, c, j], self.target(slot)
        )

    def onward(self, slot, c, j):
        at = self.unit(slot, c, j)
        return self.net.copy(
            at, at, self.sem.at[2, slot, c, j], self.sem.at[1, slot, c, j], self.net.away(node=1)
        )

    def relaying(self, slot):
        return self.receives[slot] & (self.net.me["node"] == self.near[slot])

    def send(self, source, c):
        for slot in range(2):

            @pl.when(self.sending(slot))
            def _():
                for j in range(2):
                    self.direct(source(c, j), slot, c, j).start()

    def receive(self, c):
        for slot in range(2):
            for j in range(2):
                self.onward(slot, c, j).wait_recv()

                @pl.when(self.relaying(slot))
                def _():
                    self.onward(slot, c, j).start()

    def finish(self):
        for slot in range(2):
            for c, j in itertools.product(range(2), range(2)):

                @pl.when(self.sending(slot))
                def _():
                    self.direct(self.unit(slot, c, j), slot, c, j).wait_send()

                @pl.when(self.relaying(slot))
                def _():
                    self.onward(slot, c, j).wait_send()


def kernel(
    sizes,
    ham,
    cols,
    start,
    node_re,
    node_im,
    weight_re,
    weight_im,
    sweeps,
    out,
    ham_v,
    own,
    halo_v,
    krylov,
    halo1_v,
    band_hi,
    band_lo,
    coef,
    coef_in,
    local_sem,
    halo_sem,
    halo1_sem,
    coef_sem,
    *sums,
):
    rows, width = start.shape
    half = width // 2
    net = Net(sizes)
    me, send = net.me, net.send
    position, ring = net.position, net.ring
    twin = net.away(node=1)

    ham_copy = pltpu.make_async_copy(ham, ham_v, local_sem.at[0])
    own_copy = pltpu.make_async_copy(start, own, local_sem.at[1])
    ham_copy.start()
    own_copy.start()

    peers = [net.away(**by) for by in steps_over(sizes, ("node", "x", "core"))]
    peers += [net.away(y=d) for d in range(1, sizes["y"])]
    peers += [net.away(zh=d) for d in range(1, sizes["zh"])]
    for step in (-1, 1):
        at = net.on_ring(step)
        peers += [at, {**at, "node": twin["node"]}]
    barrier = pltpu.get_barrier_semaphore()
    for peer in peers:
        pl.semaphore_signal(barrier, inc=1, device_id=peer, device_id_type=MESH)
    pl.semaphore_wait(barrier, len(peers))

    first = Halo(net, halo_v, halo_sem)
    second = Halo(net, halo1_v, halo1_sem)

    def of_start(c, j):
        return start.at[j * TILE : (j + 1) * TILE, c * half : (c + 1) * half]

    def of_krylov(c, j):
        return krylov.at[c, j * TILE : (j + 1) * TILE, :]

    for c in range(2):
        first.send(of_start, c)

    listed = [jnp.zeros((8, 128), F32) for _ in range(SWEEPS + 1)]
    for j in range(node_re.shape[0]):
        re, im = jnp.full((8, 128), node_re[j]), jnp.full((8, 128), node_im[j])
        w_re, w_im = jnp.full((8, 128), weight_re[j]), jnp.full((8, 128), weight_im[j])
        count = jnp.full((8, 128), sweeps[j])
        modulus = re * re + im * im
        inverse_re, inverse_im = re / modulus, -im / modulus
        power_re, power_im = inverse_re, inverse_im
        for degree in range(SWEEPS + 1):
            term = w_re * power_re - w_im * power_im
            listed[degree] = listed[degree] + jnp.where(count >= degree, term, 0.0)
            power_re, power_im = (
                power_re * inverse_re - power_im * inverse_im,
                power_re * inverse_im + power_im * inverse_re,
            )
    for degree, value in enumerate(listed):
        coef[8 * degree : 8 * degree + 8, :] = value
    coef_copy = send(coef, coef_in, coef_sem.at[0], coef_sem.at[1], twin)

    ham_copy.wait()
    mine = rows // TILE
    blocks = mine * ring
    for a in range(mine):
        at = position * mine + a
        offset = [
            lax.rem(cols[a, k] - at + REACH + blocks, blocks) for k in range(ham.shape[1])
        ]
        for p in range(3 * mine):
            o = p - a + REACH - mine
            total = jnp.zeros((TILE, TILE), F32)
            if 0 <= o <= 2 * REACH:
                for k in range(ham.shape[1]):
                    fixed = (REACH, 0, 2 * REACH)
                    if k < 3:
                        if fixed[k] == o:
                            total = total + ham_v[a, k]
                    else:
                        total = total + jnp.where(offset[k] == o, 1.0, 0.0) * ham_v[a, k]
            high, low = split(total)
            place = (slice(a * TILE, (a + 1) * TILE), slice(p * TILE, (p + 1) * TILE))
            band_hi[place] = high
            band_lo[place] = low

    def band(side):
        at = slice(side * rows, (side + 1) * rows)
        return band_hi[:, at], band_lo[:, at]

    own_copy.wait()
    parts = []
    for c in range(2):
        parts.append(product(band(1), split(own[:, c * half : (c + 1) * half])))
    for c in range(2):
        first.receive(c)
        total = parts[c] + product(band(0), split(halo_v[0, c]))
        total = total + product(band(2), split(halo_v[1, c]))
        krylov[c] = total
        second.send(of_krylov, c)
    coef_copy.wait_recv()
    scale = [
        (coef[8 * d : 8 * d + 8, :] + coef_in[8 * d : 8 * d + 8, :])[0:1, 0:1]
        for d in range(SWEEPS + 1)
    ]
    filtered, parts = [], []
    for c in range(2):
        total = krylov[c]
        filtered.append(scale[0] * own[:, c * half : (c + 1) * half] + scale[1] * total)
        parts.append(product(band(1), split(total)))
    for c in range(2):
        second.receive(c)
        total = parts[c] + product(band(0), split(halo1_v[0, c]))
        total = total + product(band(2), split(halo1_v[1, c]))
        filtered[c] = split(filtered[c] + scale[2] * total)

    packed = Sum(net, sums)
    for k, (a, b) in enumerate(((0, 0), (0, 1), (1, 1))):
        packed.part[k * half : (k + 1) * half, :] = product(filtered[a], filtered[b], ((0,), (0,)))
    packed.scatter()
    packed.to_y()
    packed.to_z()
    packed.gather()
    f_split = tuple(jnp.concatenate(v, axis=1) for v in zip(*filtered))
    packed.gathered()

    corner = packed.full[half : 2 * half, :]
    gram = jnp.concatenate(
        [
            jnp.concatenate([packed.full[0:half, :], corner], axis=1),
            jnp.concatenate([corner.T, packed.full[2 * half :, :]], axis=1),
        ],
        axis=0,
    )
    squares = jnp.sum(jnp.sum(gram * gram, axis=0, keepdims=True), axis=1, keepdims=True)
    norm = jnp.sqrt(squares + 1e-06)
    matrix = gram / norm
    m_split = split(matrix)
    square = product(m_split, m_split)
    mixed = product(split(square), split(0.0625 * square - 0.5625 * matrix))
    rows_at = lax.broadcasted_iota(jnp.int32, (width, width), 0)
    cols_at = lax.broadcasted_iota(jnp.int32, (width, width), 1)
    diagonal = jnp.where(rows_at == cols_at, 2.25, 0.0)
    mixed = mixed + (diagonal - 2.4375 * matrix + 1.6875 * square)
    result = product(f_split, split(mixed))
    out[...] = result * (math.sqrt(rows * ring) / jnp.sqrt(norm))

    for copy in net.sent:
        copy.wait_send()
    first.finish()
    second.finish()


def on_device(sizes, ham, cols, start, node_re, node_im, weight_re, weight_im, sweeps):
    rows, width = start.shape
    half = width // 2
    anywhere = pl.BlockSpec(memory_space=pl.ANY)
    scalars = pl.BlockSpec(memory_space=pltpu.SMEM)
    vmem = pltpu.VMEM
    dma = pltpu.SemaphoreType.DMA
    y, zh = max(sizes["y"] - 1, 1), max(sizes["zh"] - 1, 1)
    everyone = sizes["node"] * sizes["x"] * sizes["core"]

    packed = 3 * half
    piece = packed // everyone
    near = sizes["x"] * sizes["core"] - 1
    return pl.pallas_call(
        functools.partial(kernel, sizes),
        out_shape=jax.ShapeDtypeStruct((rows, width), F32),
        in_specs=[anywhere, scalars, anywhere] + [scalars] * 5,
        out_specs=pl.BlockSpec(memory_space=pltpu.VMEM),
        scratch_shapes=[
            vmem(ham.shape, F32),
            vmem((rows, width), F32),
            vmem((2, 2, rows, half), F32),
            vmem((2, rows, half), F32),
            vmem((2, 2, rows, half), F32),
            vmem((rows, 3 * rows), BF16),
            vmem((rows, 3 * rows), BF16),
            vmem((8 * (SWEEPS + 1), 128), F32),
            vmem((8 * (SWEEPS + 1), 128), F32),
            dma((2,)),
            dma((3, 2, 2, 2)),
            dma((3, 2, 2, 2)),
            dma((2,)),
            vmem((packed, half), F32),
            vmem((near, piece, half), F32),
            vmem((piece, half), F32),
            vmem((y, piece, half), F32),
            vmem((piece, half), F32),
            vmem((zh, piece, half), F32),
            vmem((packed, half), F32),
            dma((2, near)),
            dma((2, y)),
            dma((2, zh)),
            dma((2, everyone - 1)),
        ],
        compiler_params=pltpu.CompilerParams(collective_id=0, has_side_effects=True),
    )(ham, cols, start, node_re, node_im, weight_re, weight_im, sweeps)


def build(finer):
    sizes = dict(finer.shape)
    return jax.shard_map(
        functools.partial(on_device, sizes),
        mesh=finer,
        in_specs=(
            P(ROW, None, None, None),
            P(ROW, None),
            P(ROW, None),
            P("node"),
            P("node"),
            P("node"),
            P("node"),
            P("node"),
        ),
        out_specs=P(ROW, None),
        check_vma=False,
    )


def solution(mesh):
    return build(Mesh(mesh.devices.reshape(mesh.shape["node"], 4, 4, 4, 2), AXES))
```

time: 51.8 us -> 46.7 us (0.902)
  Pallas kernels: 50 us -> 44.6 us
    pallas_call x1, Pallas kernels: 50 us -> 44.6 us  [on_device(): pl.pallas_call(functools.partial(kernel, sizes), out_shape=jax.ShapeDtype...]
where the time goes in v2:
time: 46.7 us; the launch traced here: 46.3 us
  Pallas kernels  44.6 us (96%)
  local copies, waits for them, and re-layouts  1.67 us (4%)
    pallas_call x1, Pallas kernels, on_device(): pl.pallas_call(functools.partial(kernel, sizes), out_shape=jax.ShapeDtype...  44.6 us
    unnamed x1, local copies, waits for them, and re-layouts  1.67 us

profile of v2, /device:TPU:1, one launch (start us, length us, event | category | flops | bytes accessed | tf_op | source)
XLA Modules:
  0.0 46.3 jit_solution(247367449967485945)
XLA Ops:
  0.0 44.6 %shard_map.82 = f32[256,256]{1,0:T(8,128)} custom-call(f32[2,7,128,128]{3,2,1,0:T(8,128)} %ham.1, s32[2,7]{1,0:T(2,128)} %cols.1, f32[256,256]{1,0:T(8,128)} %start.1, f32[3]{0:T(128)} %node_re.1, f32[3]{0:T(128)} %node_im.1, f32[3]{0:T(128)} %weight_re.1, f32[3]{0:T(128)} %weight_im.1, s32[3]{0:T(128)} %sweeps.1), custom_call_target="tpu_custom_call" | custom-call | tf_op jit(solution)/shard_map/pallas_call | solution.py:421
  44.6 1.7 %copy.10 = f32[256,256]{1,0:T(8,128)} copy(f32[256,256]{1,0:T(8,128)} %shard_map.82) | data formatting | bytes 524288

commit v3 on v2

--- a/solution.py
+++ b/solution.py
@@ -53,7 +53,6 @@
             self.part, self.rs_in, self.y_out, self.y_in, self.z_out, self.z_in, self.full,
             self.rs_sem, self.y_sem, self.z_sem, self.ag_sem,
         ) = refs
-        self.steps = steps_over(net.sizes, ("x", "core"))
         self.everyone = steps_over(net.sizes, ("node", "x", "core"))
         self.rows = self.y_out.shape[0]
 
@@ -63,23 +62,51 @@
             index = index * self.net.sizes[axis] + at[axis]
         return pl.ds(pl.multiple_of(index * self.rows, 8), self.rows)
 
+    def partial(self, slot, by):
+        peer = self.net.away(**by)
+        landing = by["x"] * self.net.sizes["core"] + by["core"]
+        return self.net.copy(
+            self.part.at[self.piece(peer)],
+            self.rs_in.at[landing],
+            self.rs_sem.at[0, slot],
+            self.rs_sem.at[1, landing],
+            peer,
+        )
+
+    def scattering(self, by):
+        here = jnp.logical_not(self.net.far)
+        return here if by["node"] == 0 else here & self.net.edge
+
     def scatter(self):
-        self.copies = [
-            self.net.send(
-                self.part.at[self.piece(self.net.away(**by))],
-                self.rs_in.at[slot],
-                self.rs_sem.at[0, slot],
-                self.rs_sem.at[1, slot],
-                self.net.away(**by),
-            )
-            for slot, by in enumerate(self.steps)
-        ]
+        for slot, by in enumerate(self.everyone):
+
+            @pl.when(self.scattering(by))
+            def _():
+                self.partial(slot, by).start()
+
+    def finish(self):
+        for slot, by in enumerate(self.everyone):
+
+            @pl.when(self.scattering(by))
+            def _():
+                self.partial(slot, by).wait_send()
 
     def scattered(self):
-        value = self.part[self.piece(self.net.me), :]
-        for slot, copy in enumerate(self.copies):
-            copy.wait_recv()
-            value = value + self.rs_in[slot]
+        ours = self.piece(self.net.me)
+
+        def arrived(landing):
+            at = self.rs_in.at[landing]
+            self.net.copy(at, at, self.rs_sem.at[0, 0], self.rs_sem.at[1, landing], self.net.away(node=1)).wait_recv()
+
+        @pl.when(self.net.far)
+        def _():
+            arrived(0)
+            self.part[ours, :] = self.rs_in[0]
+
+        value = self.part[ours, :]
+        for landing in range(1, self.rs_in.shape[0]):
+            arrived(landing)
+            value = value + self.rs_in[landing]
         return value
 
     def share(self, value, axis, source, landing, sem):
@@ -134,6 +161,29 @@
         self.position = (
             (me["x"] * sizes["zh"] + me["zh"]) * sizes["y"] + me["y"]
         ) * sizes["core"] + me["core"]
+        head = (me["y"] == 0) & (me["core"] == 0)
+        tail = (me["y"] == sizes["y"] - 1) & (me["core"] == sizes["core"] - 1)
+        self.receives, self.sends = (head, tail), (tail, head)
+        self.near = (0, sizes["node"] - 1)
+        self.edge = head | tail
+        self.far = (head & (me["node"] != self.near[0])) | (tail & (me["node"] != self.near[1]))
+
+    def sending(self, slot):
+        return jnp.logical_not(self.sends[slot]) | (self.me["node"] != self.near[slot])
+
+    def target(self, slot):
+        node = jnp.where(self.sends[slot], self.near[slot], self.me["node"])
+        return {**self.on_ring(1 if slot == 0 else -1), "node": node}
+
+    def relaying(self, slot):
+        return self.receives[slot] & (self.me["node"] == self.near[slot])
+
+    def source(self, slot):
+        node = jnp.where(self.receives[slot], self.sizes["node"] - 1 - self.near[slot], self.me["node"])
+        return {**self.on_ring(-1 if slot == 0 else 1), "node": node}
+
+    def sourced(self, slot):
+        return jnp.logical_not(self.receives[slot]) | (self.me["node"] == self.near[slot])
 
     def away(self, **by):
         return {
@@ -172,27 +222,14 @@
 class Halo:
     def __init__(self, net, halo, sem):
         self.net, self.halo, self.sem = net, halo, sem
-        self.near = (0, net.sizes["node"] - 1)
-        me, last = net.me, {a: net.sizes[a] - 1 for a in AXES}
-        first_in_line = (me["y"] == 0) & (me["core"] == 0)
-        last_in_line = (me["y"] == last["y"]) & (me["core"] == last["core"])
-        self.receives = (first_in_line, last_in_line)
-        self.sends = (last_in_line, first_in_line)
         self.tile = halo.shape[2] // 2
-
-    def target(self, slot):
-        peer = self.net.on_ring(1 if slot == 0 else -1)
-        return {**peer, "node": jnp.where(self.sends[slot], self.near[slot], self.net.me["node"])}
-
-    def sending(self, slot):
-        return jnp.logical_not(self.sends[slot]) | (self.net.me["node"] != self.near[slot])
 
     def unit(self, slot, c, j):
         return self.halo.at[slot, c, j * self.tile : (j + 1) * self.tile, :]
 
     def direct(self, src, slot, c, j):
         return self.net.copy(
-            src, self.unit(slot, c, j), self.sem.at[0, slot, c, j], self.sem.at[1, slot, c, j], self.target(slot)
+            src, self.unit(slot, c, j), self.sem.at[0, slot, c, j], self.sem.at[1, slot, c, j], self.net.target(slot)
         )
 
     def onward(self, slot, c, j):
@@ -201,13 +238,10 @@
             at, at, self.sem.at[2, slot, c, j], self.sem.at[1, slot, c, j], self.net.away(node=1)
         )
 
-    def relaying(self, slot):
-        return self.receives[slot] & (self.net.me["node"] == self.near[slot])
-
     def send(self, source, c):
         for slot in range(2):
 
-            @pl.when(self.sending(slot))
+            @pl.when(self.net.sending(slot))
             def _():
                 for j in range(2):
                     self.direct(source(c, j), slot, c, j).start()
@@ -217,7 +251,7 @@
             for j in range(2):
                 self.onward(slot, c, j).wait_recv()
 
-                @pl.when(self.relaying(slot))
+                @pl.when(self.net.relaying(slot))
                 def _():
                     self.onward(slot, c, j).start()
 
@@ -225,11 +259,11 @@
         for slot in range(2):
             for c, j in itertools.product(range(2), range(2)):
 
-                @pl.when(self.sending(slot))
+                @pl.when(self.net.sending(slot))
                 def _():
                     self.direct(self.unit(slot, c, j), slot, c, j).wait_send()
 
-                @pl.when(self.relaying(slot))
+                @pl.when(self.net.relaying(slot))
                 def _():
                     self.onward(slot, c, j).wait_send()
 
@@ -254,10 +288,13 @@
     band_lo,
     coef,
     coef_in,
+    filt_hi,
+    filt_lo,
     local_sem,
     halo_sem,
     halo1_sem,
     coef_sem,
+    told,
     *sums,
 ):
     rows, width = start.shape
@@ -272,16 +309,32 @@
     ham_copy.start()
     own_copy.start()
 
-    peers = [net.away(**by) for by in steps_over(sizes, ("node", "x", "core"))]
-    peers += [net.away(y=d) for d in range(1, sizes["y"])]
-    peers += [net.away(zh=d) for d in range(1, sizes["zh"])]
-    for step in (-1, 1):
-        at = net.on_ring(step)
-        peers += [at, {**at, "node": twin["node"]}]
+    along = [net.away(**{a: d}) for a in ("x", "y", "zh") for d in sorted({1, sizes[a] - 1} - {0})]
+    mate = net.away(core=1)
+    peers = [mate, twin, *along]
     barrier = pltpu.get_barrier_semaphore()
+    greeted = len(peers)
+    for slot in range(2):
+
+        @pl.when(net.sourced(slot))
+        def _():
+            pl.semaphore_signal(barrier, inc=1, device_id=net.source(slot), device_id_type=MESH)
+
+        greeted = greeted + net.sending(slot).astype(jnp.int32)
     for peer in peers:
         pl.semaphore_signal(barrier, inc=1, device_id=peer, device_id_type=MESH)
-    pl.semaphore_wait(barrier, len(peers))
+    pl.semaphore_wait(barrier, greeted)
+
+    rounds = (along, [mate, twin], [mate])
+
+    def tell(at):
+        for peer in rounds[at]:
+            pl.semaphore_signal(told.at[at], inc=1, device_id=peer, device_id_type=MESH)
+
+    def hear(at):
+        if rounds[at]:
+            pl.semaphore_wait(told.at[at], len(rounds[at]))
+
 
     first = Halo(net, halo_v, halo_sem)
     second = Halo(net, halo1_v, halo1_sem)
@@ -294,6 +347,7 @@
 
     for c in range(2):
         first.send(of_start, c)
+    tell(0)
 
     listed = [jnp.zeros((8, 128), F32) for _ in range(SWEEPS + 1)]
     for j in range(node_re.shape[0]):
@@ -352,31 +406,41 @@
         total = total + product(band(2), split(halo_v[1, c]))
         krylov[c] = total
         second.send(of_krylov, c)
+        hear(c)
+        tell(c + 1)
+    hear(2)
     coef_copy.wait_recv()
     scale = [
         (coef[8 * d : 8 * d + 8, :] + coef_in[8 * d : 8 * d + 8, :])[0:1, 0:1]
         for d in range(SWEEPS + 1)
     ]
-    filtered, parts = [], []
-    for c in range(2):
-        total = krylov[c]
-        filtered.append(scale[0] * own[:, c * half : (c + 1) * half] + scale[1] * total)
-        parts.append(product(band(1), split(total)))
-    for c in range(2):
-        second.receive(c)
-        total = parts[c] + product(band(0), split(halo1_v[0, c]))
-        total = total + product(band(2), split(halo1_v[1, c]))
-        filtered[c] = split(filtered[c] + scale[2] * total)
-
+    parts = [product(band(1), split(krylov[c])) for c in range(2)]
     packed = Sum(net, sums)
-    for k, (a, b) in enumerate(((0, 0), (0, 1), (1, 1))):
-        packed.part[k * half : (k + 1) * half, :] = product(filtered[a], filtered[b], ((0,), (0,)))
+
+    def filter_rows():
+        for c in range(2):
+            second.receive(c)
+            at = slice(c * half, (c + 1) * half)
+            total = parts[c] + product(band(0), split(halo1_v[0, c]))
+            total = total + product(band(2), split(halo1_v[1, c]))
+            total = scale[0] * own[:, at] + scale[1] * krylov[c] + scale[2] * total
+            filt_hi[:, at], filt_lo[:, at] = split(total)
+
+    @pl.when(jnp.logical_not(net.far))
+    def _():
+        filter_rows()
+        halves = [
+            (filt_hi[:, c * half : (c + 1) * half], filt_lo[:, c * half : (c + 1) * half]) for c in range(2)
+        ]
+        for k, (a, b) in enumerate(((0, 0), (0, 1), (1, 1))):
+            packed.part[k * half : (k + 1) * half, :] = product(halves[a], halves[b], ((0,), (0,)))
     packed.scatter()
     packed.to_y()
     packed.to_z()
     packed.gather()
-    f_split = tuple(jnp.concatenate(v, axis=1) for v in zip(*filtered))
+    pl.when(net.far)(filter_rows)
     packed.gathered()
+    f_split = (filt_hi[...], filt_lo[...])
 
     corner = packed.full[half : 2 * half, :]
     gram = jnp.concatenate(
@@ -401,8 +465,8 @@
 
     for copy in net.sent:
         copy.wait_send()
-    first.finish()
-    second.finish()
+    for part in (first, second, packed):
+        part.finish()
 
 
 def on_device(sizes, ham, cols, start, node_re, node_im, weight_re, weight_im, sweeps):
@@ -417,7 +481,7 @@
 
     packed = 3 * half
     piece = packed // everyone
-    near = sizes["x"] * sizes["core"] - 1
+    near = sizes["x"] * sizes["core"]
     return pl.pallas_call(
         functools.partial(kernel, sizes),
         out_shape=jax.ShapeDtypeStruct((rows, width), F32),
@@ -433,10 +497,13 @@
             vmem((rows, 3 * rows), BF16),
             vmem((8 * (SWEEPS + 1), 128), F32),
             vmem((8 * (SWEEPS + 1), 128), F32),
+            vmem((rows, width), BF16),
+            vmem((rows, width), BF16),
             dma((2,)),
             dma((3, 2, 2, 2)),
             dma((3, 2, 2, 2)),
             dma((2,)),
+            pltpu.SemaphoreType.REGULAR((3,)),
             vmem((packed, half), F32),
             vmem((near, piece, half), F32),
             vmem((piece, half), F32),
@@ -444,7 +511,7 @@
             vmem((piece, half), F32),
             vmem((zh, piece, half), F32),
             vmem((packed, half), F32),
-            dma((2, near)),
+            dma((2, everyone)),
             dma((2, y)),
             dma((2, zh)),
             dma((2, everyone - 1)),

time: 46.7 us -> 44.8 us (0.959)
  Pallas kernels: 44.6 us -> 43 us
    pallas_call x1, Pallas kernels: 44.6 us -> 43 us  [on_device(): pl.pallas_call(functools.partial(kernel, sizes), out_shape=jax.ShapeDtype...]
where the time goes in v3:
time: 44.8 us; the launch traced here: 44.7 us
  Pallas kernels  43 us (96%)
  local copies, waits for them, and re-layouts  1.67 us (4%)
    pallas_call x1, Pallas kernels, on_device(): pl.pallas_call(functools.partial(kernel, sizes), out_shape=jax.ShapeDtype...  43 us
    unnamed x1, local copies, waits for them, and re-layouts  1.67 us

profile of v3, /device:TPU:1, one launch (start us, length us, event | category | flops | bytes accessed | tf_op | source)
XLA Modules:
  0.0 44.7 jit_solution(1940476570531179306)
XLA Ops:
  0.0 43.0 %shard_map.82 = f32[256,256]{1,0:T(8,128)} custom-call(f32[2,7,128,128]{3,2,1,0:T(8,128)} %ham.1, s32[2,7]{1,0:T(2,128)} %cols.1, f32[256,256]{1,0:T(8,128)} %start.1, f32[3]{0:T(128)} %node_re.1, f32[3]{0:T(128)} %node_im.1, f32[3]{0:T(128)} %weight_re.1, f32[3]{0:T(128)} %weight_im.1, s32[3]{0:T(128)} %sweeps.1), custom_call_target="tpu_custom_call" | custom-call | tf_op jit(solution)/shard_map/pallas_call | solution.py:485
  43.0 1.7 %copy.10 = f32[256,256]{1,0:T(8,128)} copy(f32[256,256]{1,0:T(8,128)} %shard_map.82) | data formatting | bytes 524288

commit v4 on v3

--- a/solution.py
+++ b/solution.py
@@ -42,8 +42,9 @@
 
 
 def steps_over(sizes, axes):
-    found = itertools.product(*(range(sizes[a]) for a in axes))
-    return [dict(zip(axes, by)) for by in found if any(by)]
+    found = [by for by in itertools.product(*(range(sizes[a]) for a in axes)) if any(by)]
+    found.sort(key=lambda by: -sum(min(d, sizes[a] - d) for a, d in zip(axes, by) if a != "core"))
+    return [dict(zip(axes, by)) for by in found]
 
 
 class Sum:
@@ -109,13 +110,17 @@
             value = value + self.rs_in[landing]
         return value
 
+    def order(self, axis):
+        size = self.net.sizes[axis]
+        return sorted(range(1, size), key=lambda d: -min(d, size - d))
+
     def share(self, value, axis, source, landing, sem):
         source[...] = value
         self.value = value
         self.landing = landing
         self.copies = [
             self.net.send(source, landing.at[d - 1], sem.at[0, d - 1], sem.at[1, d - 1], self.net.away(**{axis: d}))
-            for d in range(1, self.net.sizes[axis])
+            for d in self.order(axis)
         ]
 
     def shared(self):
@@ -166,6 +171,7 @@
         self.receives, self.sends = (head, tail), (tail, head)
         self.near = (0, sizes["node"] - 1)
         self.edge = head | tail
+        self.filling = (jnp.where(head, 1, 0), jnp.where(head, 0, 1))
         self.far = (head & (me["node"] != self.near[0])) | (tail & (me["node"] != self.near[1]))
 
     def sending(self, slot):
@@ -246,14 +252,14 @@
                 for j in range(2):
                     self.direct(source(c, j), slot, c, j).start()
 
-    def receive(self, c):
-        for slot in range(2):
-            for j in range(2):
-                self.onward(slot, c, j).wait_recv()
-
-                @pl.when(self.net.relaying(slot))
-                def _():
-                    self.onward(slot, c, j).start()
+    def receive(self, c, slot):
+        relaying = ((slot == 0) & self.net.relaying(0)) | ((slot == 1) & self.net.relaying(1))
+        for j in range(2):
+            self.onward(slot, c, j).wait_recv()
+
+            @pl.when(relaying)
+            def _():
+                self.onward(slot, c, j).start()
 
     def finish(self):
         for slot in range(2):
@@ -271,14 +277,20 @@
 def kernel(
     sizes,
     ham,
+    cols_h,
+    start,
+    node_re_h,
+    node_im_h,
+    weight_re_h,
+    weight_im_h,
+    sweeps_h,
+    out,
     cols,
-    start,
     node_re,
     node_im,
     weight_re,
     weight_im,
     sweeps,
-    out,
     ham_v,
     own,
     halo_v,
@@ -304,11 +316,6 @@
     position, ring = net.position, net.ring
     twin = net.away(node=1)
 
-    ham_copy = pltpu.make_async_copy(ham, ham_v, local_sem.at[0])
-    own_copy = pltpu.make_async_copy(start, own, local_sem.at[1])
-    ham_copy.start()
-    own_copy.start()
-
     along = [net.away(**{a: d}) for a in ("x", "y", "zh") for d in sorted({1, sizes[a] - 1} - {0})]
     mate = net.away(core=1)
     peers = [mate, twin, *along]
@@ -323,6 +330,23 @@
         greeted = greeted + net.sending(slot).astype(jnp.int32)
     for peer in peers:
         pl.semaphore_signal(barrier, inc=1, device_id=peer, device_id_type=MESH)
+    ham_copy = pltpu.make_async_copy(ham, ham_v, local_sem.at[0])
+    own_copy = pltpu.make_async_copy(start, own, local_sem.at[1])
+    few = [
+        pltpu.make_async_copy(src, dst, local_sem.at[2 + k])
+        for k, (src, dst) in enumerate(
+            (
+                (cols_h, cols),
+                (node_re_h, node_re),
+                (node_im_h, node_im),
+                (weight_re_h, weight_re),
+                (weight_im_h, weight_im),
+                (sweeps_h, sweeps),
+            )
+        )
+    ]
+    for copy in (*few, ham_copy, own_copy):
+        copy.start()
     pl.semaphore_wait(barrier, greeted)
 
     rounds = (along, [mate, twin], [mate])
@@ -349,6 +373,8 @@
         first.send(of_start, c)
     tell(0)
 
+    for copy in few:
+        copy.wait()
     listed = [jnp.zeros((8, 128), F32) for _ in range(SWEEPS + 1)]
     for j in range(node_re.shape[0]):
         re, im = jnp.full((8, 128), node_re[j]), jnp.full((8, 128), node_im[j])
@@ -388,22 +414,23 @@
                     else:
                         total = total + jnp.where(offset[k] == o, 1.0, 0.0) * ham_v[a, k]
             high, low = split(total)
-            place = (slice(a * TILE, (a + 1) * TILE), slice(p * TILE, (p + 1) * TILE))
+            side, at_p = p // mine, p % mine
+            place = (side, slice(a * TILE, (a + 1) * TILE), slice(at_p * TILE, (at_p + 1) * TILE))
             band_hi[place] = high
             band_lo[place] = low
 
     def band(side):
-        at = slice(side * rows, (side + 1) * rows)
-        return band_hi[:, at], band_lo[:, at]
+        return band_hi[side], band_lo[side]
 
     own_copy.wait()
     parts = []
     for c in range(2):
         parts.append(product(band(1), split(own[:, c * half : (c + 1) * half])))
     for c in range(2):
-        first.receive(c)
-        total = parts[c] + product(band(0), split(halo_v[0, c]))
-        total = total + product(band(2), split(halo_v[1, c]))
+        total = parts[c]
+        for slot in net.filling:
+            first.receive(c, slot)
+            total = total + product(band(2 * slot), split(halo_v[slot, c]))
         krylov[c] = total
         second.send(of_krylov, c)
         hear(c)
@@ -419,10 +446,11 @@
 
     def filter_rows():
         for c in range(2):
-            second.receive(c)
             at = slice(c * half, (c + 1) * half)
-            total = parts[c] + product(band(0), split(halo1_v[0, c]))
-            total = total + product(band(2), split(halo1_v[1, c]))
+            total = parts[c]
+            for slot in net.filling:
+                second.receive(c, slot)
+                total = total + product(band(2 * slot), split(halo1_v[slot, c]))
             total = scale[0] * own[:, at] + scale[1] * krylov[c] + scale[2] * total
             filt_hi[:, at], filt_lo[:, at] = split(total)
 
@@ -452,16 +480,18 @@
     )
     squares = jnp.sum(jnp.sum(gram * gram, axis=0, keepdims=True), axis=1, keepdims=True)
     norm = jnp.sqrt(squares + 1e-06)
-    matrix = gram / norm
-    m_split = split(matrix)
-    square = product(m_split, m_split)
-    mixed = product(split(square), split(0.0625 * square - 0.5625 * matrix))
+    scale = math.sqrt(rows * ring) / jnp.sqrt(norm)
+    by = 1.0 / norm
+    g_split = split(gram)
+    square = product(g_split, g_split) * by
+    matrix = gram * by
     rows_at = lax.broadcasted_iota(jnp.int32, (width, width), 0)
     cols_at = lax.broadcasted_iota(jnp.int32, (width, width), 1)
-    diagonal = jnp.where(rows_at == cols_at, 2.25, 0.0)
-    mixed = mixed + (diagonal - 2.4375 * matrix + 1.6875 * square)
-    result = product(f_split, split(mixed))
-    out[...] = result * (math.sqrt(rows * ring) / jnp.sqrt(norm))
+    diagonal = jnp.where(rows_at == cols_at, 2.25 * scale, 0.0)
+    square = square * by
+    low = diagonal - (2.4375 * scale) * matrix + (1.6875 * scale) * square
+    mixed = low + product(split(square), split((0.0625 * scale) * square - (0.5625 * scale) * matrix))
+    out[...] = product(f_split, split(mixed))
 
     for copy in net.sent:
         copy.wait_send()
@@ -473,7 +503,7 @@
     rows, width = start.shape
     half = width // 2
     anywhere = pl.BlockSpec(memory_space=pl.ANY)
-    scalars = pl.BlockSpec(memory_space=pltpu.SMEM)
+    smem = pltpu.SMEM
     vmem = pltpu.VMEM
     dma = pltpu.SemaphoreType.DMA
     y, zh = max(sizes["y"] - 1, 1), max(sizes["zh"] - 1, 1)
@@ -482,24 +512,31 @@
     packed = 3 * half
     piece = packed // everyone
     near = sizes["x"] * sizes["core"]
+    ham, cols, start, node_re, node_im, weight_re, weight_im, sweeps = (
+        pltpu.with_memory_space_constraint(v, pltpu.HBM)
+        for v in (ham, cols, start, node_re, node_im, weight_re, weight_im, sweeps)
+    )
     return pl.pallas_call(
         functools.partial(kernel, sizes),
         out_shape=jax.ShapeDtypeStruct((rows, width), F32),
-        in_specs=[anywhere, scalars, anywhere] + [scalars] * 5,
+        in_specs=[anywhere] * 8,
         out_specs=pl.BlockSpec(memory_space=pltpu.VMEM),
         scratch_shapes=[
+            smem(cols.shape, jnp.int32),
+            *[smem(v.shape, F32) for v in (node_re, node_im, weight_re, weight_im)],
+            smem(sweeps.shape, jnp.int32),
             vmem(ham.shape, F32),
             vmem((rows, width), F32),
             vmem((2, 2, rows, half), F32),
             vmem((2, rows, half), F32),
             vmem((2, 2, rows, half), F32),
-            vmem((rows, 3 * rows), BF16),
-            vmem((rows, 3 * rows), BF16),
+            vmem((3, rows, rows), BF16),
+            vmem((3, rows, rows), BF16),
             vmem((8 * (SWEEPS + 1), 128), F32),
             vmem((8 * (SWEEPS + 1), 128), F32),
             vmem((rows, width), BF16),
             vmem((rows, width), BF16),
-            dma((2,)),
+            dma((8,)),
             dma((3, 2, 2, 2)),
             dma((3, 2, 2, 2)),
             dma((2,)),
@@ -516,7 +553,7 @@
             dma((2, zh)),
             dma((2, everyone - 1)),
         ],
-        compiler_params=pltpu.CompilerParams(collective_id=0, has_side_effects=True),
+        compiler_params=pltpu.CompilerParams(collective_id=0, has_side_effects=True, vmem_limit_bytes=40 * 1024 * 1024),
     )(ham, cols, start, node_re, node_im, weight_re, weight_im, sweeps)
 
 

time: 44.8 us -> 41.7 us (0.931)
  Pallas kernels: 43 us -> 40.9 us
  local copies, waits for them, and re-layouts: 1.67 us -> 0.71 us
    pallas_call x1, Pallas kernels: 43 us -> 40.9 us  [on_device(): pl.pallas_call(functools.partial(kernel, sizes), out_shape=jax.ShapeDtype...]
    unnamed x1, local copies, waits for them, and re-layouts: 1.67 us -> 0.71 us
where the time goes in v4:
time: 41.7 us; the launch traced here: 41.6 us
  Pallas kernels  40.9 us (98%)
  local copies, waits for them, and re-layouts  0.71 us (2%)
    pallas_call x1, Pallas kernels, on_device(): pl.pallas_call(functools.partial(kernel, sizes), out_shape=jax.ShapeDtype...  40.9 us

profile of v4, /device:TPU:1, one launch (start us, length us, event | category | flops | bytes accessed | tf_op | source)
XLA Modules:
  0.0 41.6 jit_solution(256475658575856808)
XLA Ops:
  0.0 40.9 %shard_map.82 = f32[256,256]{1,0:T(8,128)S(1)} custom-call(f32[2,7,128,128]{3,2,1,0:T(8,128)} %ham.1, s32[2,7]{1,0:T(2,128)} %cols_h.1, f32[256,256]{1,0:T(8,128)} %start.1, f32[3]{0:T(128)} %node_re_h.1, f32[3]{0:T(128)} %node_im_h.1, f32[3]{0:T(128)} %weight_re_h.1, f32[3]{0:T(128)} %weight_im_h.1, s32[3]{0:T(128)} %sweeps_h.1), custom_call_target="tpu_custom_call" | custom-call | tf_op jit(solution)/shard_map/pallas_call | solution.py:519
  40.9 0.7 %copy.10 = f32[256,256]{1,0:T(8,128)} copy(f32[256,256]{1,0:T(8,128)S(1)} %shard_map.82) | data formatting | bytes 524288

commit v5 on v4

--- a/solution.py
+++ b/solution.py
@@ -128,11 +128,11 @@
             copy.wait_recv()
         return pairwise([self.value] + [self.landing[d] for d in range(len(self.copies))])
 
+    def to_z(self):
+        self.share(self.scattered(), "zh", self.z_out, self.z_in, self.z_sem)
+
     def to_y(self):
-        self.share(self.scattered(), "y", self.y_out, self.y_in, self.y_sem)
-
-    def to_z(self):
-        self.share(self.shared(), "zh", self.z_out, self.z_in, self.z_sem)
+        self.share(self.shared(), "y", self.y_out, self.y_in, self.y_sem)
 
     def gather(self):
         value = self.shared()
@@ -226,8 +226,8 @@
 
 
 class Halo:
-    def __init__(self, net, halo, sem):
-        self.net, self.halo, self.sem = net, halo, sem
+    def __init__(self, net, halo, sem, later=False):
+        self.net, self.halo, self.sem, self.later = net, halo, sem, later
         self.tile = halo.shape[2] // 2
 
     def unit(self, slot, c, j):
@@ -257,7 +257,16 @@
         for j in range(2):
             self.onward(slot, c, j).wait_recv()
 
-            @pl.when(relaying)
+            if not self.later:
+
+                @pl.when(relaying)
+                def _():
+                    self.onward(slot, c, j).start()
+
+    def relay(self):
+        for slot, c, j in itertools.product(range(2), range(2), range(2)):
+
+            @pl.when(self.net.relaying(slot))
             def _():
                 self.onward(slot, c, j).start()
 
@@ -361,7 +370,7 @@
 
 
     first = Halo(net, halo_v, halo_sem)
-    second = Halo(net, halo1_v, halo1_sem)
+    second = Halo(net, halo1_v, halo1_sem, later=True)
 
     def of_start(c, j):
         return start.at[j * TILE : (j + 1) * TILE, c * half : (c + 1) * half]
@@ -463,8 +472,9 @@
         for k, (a, b) in enumerate(((0, 0), (0, 1), (1, 1))):
             packed.part[k * half : (k + 1) * half, :] = product(halves[a], halves[b], ((0,), (0,)))
     packed.scatter()
+    second.relay()
+    packed.to_z()
     packed.to_y()
-    packed.to_z()
     packed.gather()
     pl.when(net.far)(filter_rows)
     packed.gathered()

time: 41.7 us -> 41.4 us (level)
  no operation moved by 1% of the time
where the time goes in v5:
time: 41.4 us; the launch traced here: 41.3 us
  Pallas kernels  40.6 us (98%)
  local copies, waits for them, and re-layouts  0.71 us (2%)
    pallas_call x1, Pallas kernels, on_device(): pl.pallas_call(functools.partial(kernel, sizes), out_shape=jax.ShapeDtype...  40.6 us

profile of v5, /device:TPU:1, one launch (start us, length us, event | category | flops | bytes accessed | tf_op | source)
XLA Modules:
  0.0 41.3 jit_solution(17839372346708699623)
XLA Ops:
  0.0 40.6 %shard_map.82 = f32[256,256]{1,0:T(8,128)S(1)} custom-call(f32[2,7,128,128]{3,2,1,0:T(8,128)} %ham.1, s32[2,7]{1,0:T(2,128)} %cols_h.1, f32[256,256]{1,0:T(8,128)} %start.1, f32[3]{0:T(128)} %node_re_h.1, f32[3]{0:T(128)} %node_im_h.1, f32[3]{0:T(128)} %weight_re_h.1, f32[3]{0:T(128)} %weight_im_h.1, s32[3]{0:T(128)} %sweeps_h.1), custom_call_target="tpu_custom_call" | custom-call | tf_op jit(solution)/shard_map/pallas_call | solution.py:529
  40.6 0.7 %copy.10 = f32[256,256]{1,0:T(8,128)} copy(f32[256,256]{1,0:T(8,128)S(1)} %shard_map.82) | data formatting | bytes 524288
